TPU v7x, 256 devices: a whole 4x4x8 slice. The times are simulated.
256 devices in a mesh: space: 32 (over z, y_lo, core), tm: 4 (over x), cores: 2 (over y_hi).
Axes of the slice: x: 4, y: 4 (y_hi: 2, y_lo: 2; y = y_hi * 2 + y_lo), z: 8, core: 2. Of those that a mesh axis runs over, the one named last changes fastest.
Arguments:
- initial_state: float32 [1024, 64, 512], P('space', 'cores'), may hold values from -6 to 6
- heat_source: float32 [1024, 64, 512], P('space', 'cores'), may hold values from -3 to 3
- source_amplitude: float32 [32], P('tm'), may hold values from 0.5 to 1.5
- diffusivity: float32 [32], P('space'), may hold values from 0.5 to 2
- robin_param: float32 [32], P('space'), may hold values from 0.5 to 4
- spectrum_x: float32 [32], replicated, may hold values from 0.002 to 0.38
- spectrum_y: float32 [64], P('cores'), may hold values from 0.002 to 0.38
- spectrum_z: float32 [512], replicated, may hold values from 0.002 to 0.38
- robin_in: float32 [32, 2, 32, 64, 512], P('space', None, 'tm', 'cores'), may hold values from -8 to 8
- open_flag: int32 [32, 64], P(None, 'cores'), may hold values from 0 to 1, as said below
- owner_side: int32 [32, 64], P(None, 'cores'), may hold values from 0 to 1, as said below
Outputs:
- robin_out: float32 [32, 2, 32, 64, 512], P('space', None, 'tm', 'cores')
- window_end: float32 [4, 1024, 64, 512], P('tm', 'space', 'cores')
Inputs may be any that keep to these rules, and one draw needn't show every extreme that they name: In each aligned group of 4 modes b of an interface exactly one has open_flag 0. In each aligned pair of modes b of an interface exactly one has owner_side 1.
All inputs are finite; a program needn't handle non-finite values.
Results may differ from a plain program's by a relative error of at most 0.00015.
Values sent between devices are 32-bit elements; how exact they have to be, the bound alone decides.
A program may use at most 128 MiB of HBM per device.

v0:
```python
import jax
import jax.numpy as jnp
from jax import lax
from jax.sharding import PartitionSpec as P

HIGHEST = lax.Precision.HIGHEST


def passed_along(block, axis, distance):
    devices = range(lax.axis_size(axis))
    route = [(i - distance, i) for i in devices if i - distance in devices]
    return lax.ppermute(block, axis, route)


def passed_along_2(x, axis, by):
    devices = lax.axis_size(axis)
    return lax.ppermute(x, axis, [(i, (i + by) % devices) for i in range(devices)])


def cosine_basis(order):
    mode_rows = jnp.arange(order, dtype=jnp.float32)[:, None]
    node_cols = jnp.arange(order, dtype=jnp.float32)[None, :]
    scaling = jnp.where(mode_rows == 0, jnp.sqrt(1.0 / order), jnp.sqrt(2.0 / order))
    return scaling * jnp.cos(jnp.pi * mode_rows * (node_cols + 0.5) / order)


def local(
    initial_state,
    heat_source,
    source_amplitude,
    diffusivity,
    robin_param,
    spectrum_x,
    spectrum_y,
    spectrum_z,
    robin_in,
    open_flag,
    owner_side,
):
    nodes_x, half_y, nodes_z = initial_state.shape
    nodes_y = half_y * lax.axis_size("cores")
    core_index = lax.axis_index("cores")
    basis_x = cosine_basis(nodes_x)
    basis_y = cosine_basis(nodes_y)
    basis_z = cosine_basis(nodes_z)
    mode_block = lax.dynamic_slice_in_dim(basis_y, core_index * half_y, half_y, 0)
    node_block = lax.dynamic_slice_in_dim(basis_y, core_index * half_y, half_y, 1)

    def local_forward(values):
        values = jnp.einsum("ax,xyz->ayz", basis_x, values, precision=HIGHEST)
        return jnp.einsum("cz,ayz->ayc", basis_z, values, precision=HIGHEST)

    pieces = (
        lax.all_gather(local_forward(initial_state), "cores", axis=1, tiled=True),
        lax.all_gather(local_forward(heat_source), "cores", axis=1, tiled=True),
    )
    start_modes, source_modes = tuple(
        (
            jnp.einsum("by,ayc->abc", mode_block, piece_part, precision=HIGHEST)
            for piece_part in pieces
        )
    )
    rates = spectrum_x[:, None, None] + spectrum_y[None, :, None] + spectrum_z[None, None, :]
    factor = 1.0 / (1.0 + diffusivity[0] * rates)
    edge_rows = jnp.stack(
        [
            basis_x[:, 0],
            basis_x[:, 1] - basis_x[:, 0],
            basis_x[:, nodes_x - 1],
            basis_x[:, nodes_x - 1] - basis_x[:, nodes_x - 2],
        ]
    )
    left_col = basis_x[:, 0][:, None, None]
    right_col = basis_x[:, nodes_x - 1][:, None, None]
    robin_here = robin_in[0]
    steps_here = source_amplitude.shape[0]
    windows = lax.axis_size("tm")
    tm_index = lax.axis_index("tm")
    opening = start_modes
    for window in range(windows):
        current = opening
        collected = []
        for substep in range(steps_here):
            forcing = current
            forcing = forcing + source_amplitude[substep] * source_modes
            forcing = (
                forcing
                + left_col * robin_here[0, substep][None]
                + right_col * robin_here[1, substep][None]
            )
            current = forcing * factor
            collected.append(jnp.einsum("ka,abc->kbc", edge_rows, current, precision=HIGHEST))
        closing = current
        traces = jnp.stack(collected)
        if window + 1 < windows:
            passed = passed_along(closing, "tm", 1)
            opening = jnp.where(tm_index == 0, start_modes, passed)
    subdomains = lax.axis_size("space")
    space_index = lax.axis_index("space")
    left_index = (space_index + subdomains - 1) % subdomains
    open_right = open_flag[space_index].astype(jnp.float32)[:, None]
    open_left = open_flag[left_index].astype(jnp.float32)[:, None]
    side_right = owner_side[space_index][:, None]
    side_left = owner_side[left_index][:, None]
    owns_right = side_right == 0
    owns_left = side_left == 1
    left_face = traces[:, 0:2]
    right_face = traces[:, 2:4]
    send_left = jnp.where(side_left == 0, left_face, 0.0)
    send_right = jnp.where(side_right == 1, right_face, 0.0)
    got_right = passed_along_2(send_left, "space", -1)
    got_left = passed_along_2(send_right, "space", 1)
    own_right_data = open_right * (got_right[:, 1] + robin_param[0] * got_right[:, 0])
    own_left_data = open_left * (robin_param[0] * got_left[:, 0] - got_left[:, 1])
    back_right = jnp.where(
        owns_right, open_right * (robin_param[0] * right_face[:, 0] - right_face[:, 1]), 0.0
    )
    back_left = jnp.where(
        owns_left, open_left * (left_face[:, 1] + robin_param[0] * left_face[:, 0]), 0.0
    )
    returned_left = passed_along_2(back_right, "space", 1)
    returned_right = passed_along_2(back_left, "space", -1)
    left_data = jnp.where(owns_left, own_left_data, returned_left)
    right_data = jnp.where(owns_right, own_right_data, returned_right)
    robin_out = jnp.stack([left_data, right_data])[None]
    spectral = jnp.einsum("ax,abc->xbc", basis_x, closing, precision=HIGHEST)
    spectral = jnp.einsum("cz,xbc->xbz", basis_z, spectral, precision=HIGHEST)
    physical = jnp.einsum(
        "by,xbz->xyz",
        node_block,
        lax.all_gather(spectral, "cores", axis=1, tiled=True),
        precision=HIGHEST,
    )
    return (robin_out, physical[None])


def solution(mesh):
    placed = (
        P("space", "cores", None),
        P("space", "cores", None),
        P("tm"),
        P("space"),
        P("space"),
        P(),
        P("cores"),
        P(),
        P("space", None, "tm", "cores", None),
        P(None, "cores"),
        P(None, "cores"),
    )
    return jax.shard_map(
        local,
        mesh=mesh,
        in_specs=placed,
        out_specs=(P("space", None, "tm", "cores", None), P("tm", "space", "cores", None)),
        check_vma=False,
    )
```

profile of v0, /device:TPU:3, one launch (start us, length us, event | category | flops | bytes accessed | tf_op | source)
XLA Modules:
  0.0 476.9 jit_solution(9938863236364807262)
XLA Ops:
  7.2 0.0 copy-start
  7.2 0.0 all-gather.6.cloned.1.call-start
  7.3 1.5 copy-done
  8.8 3.1 fusion.57
  11.9 10.7 %fusion.55 = f32[32,32,512]{2,1,0:T(8,128)} fusion(f32[32,32,512]{2,0,1:T(8,128)S(1)} %fusion.57, f32[512]{0:T(512)S(1)} %get-tuple-element.57, f32[512]{0:T(512)S(1)} %get-tuple-element.58, f32[512]{0:T(512)S(1)} %fusion.181), kind=kOutput, calls=%fused_computation.133 | convolution fusion | flops 3222011904 | bytes 4200448 | tf_op jit(solution)/shard_map/cz,ayz->ayc/dot_general | solution.py:51
  22.6 0.0 all-gather.6.cloned.1.call-update
  22.6 0.3 all-gather.4.cloned.1.call-start
  23.0 4.7 fusion.61
  27.6 10.7 %fusion.59 = f32[32,32,512]{2,1,0:T(8,128)} fusion(f32[32,32,512]{2,0,1:T(8,128)S(1)} %fusion.61, f32[512]{0:T(512)S(1)} %get-tuple-element.57, f32[512]{0:T(512)S(1)} %get-tuple-element.58, f32[512]{0:T(512)S(1)} %fusion.181), kind=kOutput, calls=%fused_computation.137 | convolution fusion | flops 3222011904 | bytes 4200448 | tf_op jit(solution)/shard_map/cz,ayz->ayc/dot_general | solution.py:51
  38.4 0.0 all-gather.4.cloned.1.call-update
  38.4 0.6 all-gather.8.cloned.1.call-start
  39.6 0.7 fusion.206
  40.3 0.1 cosine_multiply_fusion.5
  40.5 0.0 copy-done.14
  40.5 0.0 copy-done.15
  40.5 0.1 broadcast_add_fusion
  40.6 0.2 cosine_multiply_fusion.4
  40.8 0.1 slice_bitcast_fusion.15
  40.9 0.0 copy-start.13
  40.9 48.2 %all-gather.6.cloned.1.call-done = f32[32,64,512]{2,1,0:T(8,128)} async-done(((f32[32,32,512]{2,1,0:T(8,128)}), f32[32,64,512]{2,1,0:T(8,128)}) %all-gather.6.cloned.1.call-update) | async-done | bytes 4194320 | tf_op jit(solution)/shard_map/all_gather | solution.py:55
  89.1 4.2 fusion.160
  93.2 60.5 %all-gather.4.cloned.1.call-done = f32[32,64,512]{2,1,0:T(8,128)} async-done(((f32[32,32,512]{2,1,0:T(8,128)}), f32[32,64,512]{2,1,0:T(8,128)}) %all-gather.4.cloned.1.call-update) | async-done | bytes 4194320 | tf_op jit(solution)/shard_map/all_gather | solution.py:54
  153.7 14.2 %fusion.49 = (f32[32,32,512]{2,1,0:T(8,128)}, f32[32,512,32]{1,2,0:T(8,128)}) fusion(f32[32,512,32]{1,2,0:T(8,128)S(1)} %fusion.160, f32[32,512]{1,0:T(8,128)S(1)} %get-tuple-element.16, f32[32,512]{1,0:T(8,128)S(1)} %get-tuple-element.17, f32[]{:T(128)} %bitcast.45, f32[32,512]{1,0:T(8,128)S(1)} %get-tuple-element.18, ...), kind=kOutput, calls=%fused_computation.113 | convolution fusion | flops 434110464 | bytes 11570216 | tf_op jit(solution)/shard_map/by,ayc->abc/dot_general | solution.py:59
  167.9 3.1 collective-permute-start
  171.0 45.6 %collective-permute-done = f32[32,32,512]{2,1,0:T(8,128)} collective-permute-done((f32[32,32,512]{2,1,0:T(8,128)}, f32[32,32,512]{2,1,0:T(8,128)}, u32[]{:S(2)}, u32[]{:S(2)}) %collective-permute-start) | collective-permute-done | bytes 2097184 | tf_op jit(solution)/shard_map/ppermute | solution.py:12
  216.6 11.1 %fusion.50 = f32[32,32,512]{2,1,0:T(8,128)S(1)} fusion(f32[32,32,512]{2,1,0:T(8,128)} %collective-permute-done, f32[32,512,32]{1,2,0:T(8,128)} %get-tuple-element.54, f32[32,512,32]{1,2,0:T(8,128)S(1)} %fusion.160, f32[32,512]{1,0:T(8,128)S(1)} %get-tuple-element.16, f32[32,512]{1,0:T(8,128)S(1)} %get-tuple-element.17, f32[]{:T(128)} %bitcast.45, ...), kind=kLoop, calls=%fused_computation.114 | loop fusion | flops 31981568 | bytes 9443621 | tf_op jit(solution)/shard_map/mul | solution.py:91
  227.7 3.1 collective-permute-start.1
  230.8 44.4 %collective-permute-done.1 = f32[32,32,512]{2,1,0:T(8,128)S(1)} collective-permute-done((f32[32,32,512]{2,1,0:T(8,128)S(1)}, f32[32,32,512]{2,1,0:T(8,128)S(1)}, u32[]{:S(2)}, u32[]{:S(2)}) %collective-permute-start.1) | collective-permute-done | bytes 2097184 | tf_op jit(solution)/shard_map/ppermute | solution.py:12
  275.2 10.5 %fusion.51 = f32[32,32,512]{2,1,0:T(8,128)} fusion(f32[32,32,512]{2,1,0:T(8,128)S(1)} %collective-permute-done.1, f32[32,512,32]{1,2,0:T(8,128)S(1)} %copy-done.4, f32[32,512,32]{1,2,0:T(8,128)S(1)} %fusion.160, f32[32,512]{1,0:T(8,128)S(1)} %get-tuple-element.16, f32[32,512]{1,0:T(8,128)S(1)} %get-tuple-element.17, f32[]{:T(128)} %bitcast.45, ...), kind=kLoop, calls=%fused_computation.115 | loop fusion | flops 31981568 | bytes 9443621 | tf_op jit(solution)/shard_map/mul | solution.py:91
  285.7 3.1 collective-permute-start.2
  289.4 0.8 fusion.188
  290.2 0.8 compare_bitcast_fusion.2
  291.0 41.6 %collective-permute-done.2 = f32[32,32,512]{2,1,0:T(8,128)} collective-permute-done((f32[32,32,512]{2,1,0:T(8,128)}, f32[32,32,512]{2,1,0:T(8,128)}, u32[]{:S(2)}, u32[]{:S(2)}) %collective-permute-start.2) | collective-permute-done | bytes 2097184 | tf_op jit(solution)/shard_map/ppermute | solution.py:12
  332.5 14.2 %fusion.52 = (f32[32,32,512]{2,1,0:T(8,128)S(1)}, f32[32,32,512]{2,1,0:T(8,128)}, f32[32,32,512]{2,1,0:T(8,128)}, f32[32,32,512]{2,1,0:T(8,128)}, f32[32,32,512]...) fusion(f32[32,512,32]{1,2,0:T(8,128)S(1)} %fusion.160, ...), kind=kLoop, calls=%fused_computation.116 | loop fusion | flops 31981568 | bytes 24123684 | tf_op jit(solution)/shard_map/mul | solution.py:91
  346.8 3.1 fusion.77
  349.9 9.4 %fusion.53 = f32[32,32,512]{2,1,0:T(8,128)} fusion(f32[32,32,512]{2,0,1:T(8,128)S(1)} %fusion.77, f32[512]{0:T(512)S(1)} %get-tuple-element.57, f32[512]{0:T(512)S(1)} %get-tuple-element.58, f32[512]{0:T(512)S(1)} %fusion.181), kind=kOutput, calls=%fused_computation.131 | convolution fusion | flops 3222011904 | bytes 4200448 | tf_op jit(solution)/shard_map/cz,xbc->xbz/dot_general | solution.py:127
  359.3 0.0 all-gather.8.cloned.1.call-update
  359.4 4.1 fusion.90
  363.5 2.3 fusion.96
  365.8 2.3 fusion.102
  368.1 2.3 fusion.108
  370.5 0.0 copy-start.5
  370.5 2.3 fusion.114
  372.8 2.7 fusion.120
  375.5 2.3 fusion.126
  377.8 2.3 fusion.84
  380.1 1.0 fusion.204
  381.1 0.3 copy_select_fusion.1
  381.4 3.7 collective-permute-start.3
  385.1 1.3 fusion.205
  386.4 0.2 fusion.144
  386.6 0.1 collective-permute-start.4
  386.7 0.3 copy_select_fusion
  387.0 0.6 collective-permute-start.5
  387.5 65.4 %collective-permute-done.4 = f32[8,32,512]{2,1,0:T(8,128)S(1)} collective-permute-done((f32[8,32,512]{2,1,0:T(8,128)S(1)}, f32[8,32,512]{2,1,0:T(8,128)S(1)}, u32[]{:S(2)}, u32[]{:S(2)}) %collective-permute-start.4) | collective-permute-done | bytes 524320 | tf_op jit(solution)/shard_map/ppermute | solution.py:17
  453.0 0.0 collective-permute-done.3
  453.0 0.3 fusion.141
  453.3 0.3 collective-permute-start.6
  453.5 0.0 collective-permute-done.5
  453.6 9.3 %collective-permute-done.6 = f32[8,32,512]{2,1,0:T(8,128)S(1)} collective-permute-done((f32[8,32,512]{2,1,0:T(8,128)S(1)}, f32[8,32,512]{2,1,0:T(8,128)S(1)}, u32[]{:S(2)}, u32[]{:S(2)}) %collective-permute-start.6) | collective-permute-done | bytes 524320 | tf_op jit(solution)/shard_map/ppermute | solution.py:17
  462.9 0.2 fusion.137
  463.1 0.0 copy-start.1
  463.1 1.1 maximum_bitcast_fusion
  464.2 6.0 %convolution_bitcast_fusion = f32[1,32,32,512]{3,2,1,0:T(8,128)} fusion(f32[32,64,512]{2,1,0:T(8,128)} %all-gather.8.cloned.1.call-done, f32[64,64]{1,0:T(8,128)S(1)} %cosine_multiply_fusion.4, s32[]{:T(128)S(6)} %select_n.140), kind=kOutput, calls=%fused_computation.160 | convolution fusion | flops 402653184 | bytes 6307844 | tf_op jit(solution)/shard_map/by,xbz->xyz/dot_general | solution.py:128
  (34 shorter events, 0.1 us)
Async XLA Ops:
  7.2 1.6 copy-start
  7.2 81.9 %all-gather.6.cloned.1.call-start = ((), (), s32[]{:S(2)}) async-start(), calls=%async_computation.1 | async-start | bytes 6291456 | tf_op jit(solution)/shard_map/all_gather | solution.py:55
  22.6 131.1 %all-gather.4.cloned.1.call-start = ((), (), s32[]{:S(2)}) async-start(), calls=%async_computation | async-start | bytes 6291456 | tf_op jit(solution)/shard_map/all_gather | solution.py:54
  38.3 1.3 copy-start.12
  38.3 2.1 copy-start.14
  38.3 2.1 copy-start.15
  38.3 2.4 copy-start.11
  38.4 425.8 %all-gather.8.cloned.1.call-start = ((), (), s32[]{:S(2)}) async-start(), calls=%async_computation.2 | async-start | bytes 6291456 | tf_op jit(solution)/shard_map/all_gather | solution.py:131
  40.9 112.9 %copy-start.13 = (f32[512]{0:T(512)S(1)}, f32[512]{0:T(512)}, u32[]{:S(2)}) copy-start(f32[512]{0:T(512)} %param.18) | copy-start | bytes 6148
  167.9 48.7 %collective-permute-start = (f32[32,32,512]{2,1,0:T(8,128)}, f32[32,32,512]{2,1,0:T(8,128)}, u32[]{:S(2)}, u32[]{:S(2)}) collective-permute-start(f32[32,32,512]{2,1,0:T(8,128)} %get-tuple-element.53), channel_id=1, source_target_pairs={{0,2},{2,4},{4,6},{1,3},{3,5},{5,7},{8,10},{10,12},{12,14},{9,11},... | collective-permute-start | bytes 6291464 | tf_op jit(solution)/shard_map/ppermute | solution.py:12
  216.6 58.6 %copy-start.4 = (f32[32,512,32]{1,2,0:T(8,128)S(1)}, f32[32,512,32]{1,2,0:T(8,128)}, u32[]{:S(2)}) copy-start(f32[32,512,32]{1,2,0:T(8,128)} %get-tuple-element.54) | copy-start | bytes 6291460
  227.7 47.5 %collective-permute-start.1 = (f32[32,32,512]{2,1,0:T(8,128)S(1)}, f32[32,32,512]{2,1,0:T(8,128)S(1)}, u32[]{:S(2)}, u32[]{:S(2)}) collective-permute-start(f32[32,32,512]{2,1,0:T(8,128)S(1)} %fusion.50), channel_id=1, source_target_pairs={{0,2},{2,4},{4,6},{1,3},{3,5},{5,7},{8,10},{10,12},{12,14},{9,11},... | collective-permute-start | bytes 6291464 | tf_op jit(solution)/shard_map/ppermute | solution.py:12
  285.7 46.9 %collective-permute-start.2 = (f32[32,32,512]{2,1,0:T(8,128)}, f32[32,32,512]{2,1,0:T(8,128)}, u32[]{:S(2)}, u32[]{:S(2)}) collective-permute-start(f32[32,32,512]{2,1,0:T(8,128)} %fusion.51), channel_id=1, source_target_pairs={{0,2},{2,4},{4,6},{1,3},{3,5},{5,7},{8,10},{10,12},{12,14},{9,11},... | collective-permute-start | bytes 6291464 | tf_op jit(solution)/shard_map/ppermute | solution.py:12
  346.7 3.1 copy-start.2
  359.3 4.2 copy-start.10
  359.3 6.5 %copy-start.9 = (f32[32,32,512]{2,1,0:T(8,128)S(1)}, f32[32,32,512]{2,1,0:T(8,128)}, u32[]{:S(2)}) copy-start(f32[32,32,512]{2,1,0:T(8,128)} %get-tuple-element.7) | copy-start | bytes 6291460
  363.5 4.6 copy-start.8
  365.8 4.6 copy-start.7
  368.1 4.6 copy-start.6
  370.5 5.0 %copy-start.5 = (f32[32,32,512]{2,1,0:T(8,128)S(1)}, f32[32,32,512]{2,1,0:T(8,128)}, u32[]{:S(2)}) copy-start(f32[32,32,512]{2,1,0:T(8,128)} %get-tuple-element.3) | copy-start | bytes 6291460
  372.8 5.0 %copy-start.3 = (f32[32,32,512]{2,1,0:T(8,128)S(1)}, f32[32,32,512]{2,1,0:T(8,128)}, u32[]{:S(2)}) copy-start(f32[32,32,512]{2,1,0:T(8,128)} %copy-done.2) | copy-start | bytes 6291460
  381.4 71.5 %collective-permute-start.3 = (f32[8,2,32,512]{3,2,0,1:T(8,128)S(1)}, f32[8,2,32,512]{3,2,0,1:T(8,128)S(1)}, u32[]{:S(2)}, u32[]{:S(2)}) collective-permute-start(f32[8,2,32,512]{3,2,0,1:T(8,128)S(1)} %copy_select_fusion.1), channel_id=1, source_target_pairs={{0,8},{8,16},{16,24},{24,32},{32,40},{40,48},{48,56},{56,64},{64,7... | collective-permute-start | bytes 3145736 | tf_op jit(solution)/shard_map/ppermute | solution.py:17
  386.6 66.4 %collective-permute-start.4 = (f32[8,32,512]{2,1,0:T(8,128)S(1)}, f32[8,32,512]{2,1,0:T(8,128)S(1)}, u32[]{:S(2)}, u32[]{:S(2)}) collective-permute-start(f32[8,32,512]{2,1,0:T(8,128)S(1)} %fusion.144), channel_id=1, source_target_pairs={{0,8},{8,16},{16,24},{24,32},{32,40},{40,48},{48,56},{56,64},{64,7... | collective-permute-start | bytes 1572872 | tf_op jit(solution)/shard_map/ppermute | solution.py:17
  387.0 66.6 %collective-permute-start.5 = (f32[8,2,32,512]{3,2,0,1:T(8,128)S(1)}, f32[8,2,32,512]{3,2,0,1:T(8,128)S(1)}, u32[]{:S(2)}, u32[]{:S(2)}) collective-permute-start(f32[8,2,32,512]{3,2,0,1:T(8,128)S(1)} %copy_select_fusion), channel_id=1, source_target_pairs={{0,248},{8,0},{16,8},{24,16},{32,24},{40,32},{48,40},{56,48},{64,5... | collective-permute-start | bytes 3145736 | tf_op jit(solution)/shard_map/ppermute | solution.py:17
  453.3 9.6 %collective-permute-start.6 = (f32[8,32,512]{2,1,0:T(8,128)S(1)}, f32[8,32,512]{2,1,0:T(8,128)S(1)}, u32[]{:S(2)}, u32[]{:S(2)}) collective-permute-start(f32[8,32,512]{2,1,0:T(8,128)S(1)} %get-tuple-element.44), channel_id=1, source_target_pairs={{0,248},{8,0},{16,8},{24,16},{32,24},{40,32},{48,40},{56,48},{64,5... | collective-permute-start | bytes 1572872 | tf_op jit(solution)/shard_map/ppermute | solution.py:17
  463.1 7.1 %copy-start.1 = (f32[32,32,512]{2,1,0:T(8,128)S(1)}, f32[32,32,512]{2,1,0:T(8,128)}, u32[]{:S(2)}) copy-start(f32[32,32,512]{2,1,0:T(8,128)} %param.12) | copy-start | bytes 6291460
Sparse Core Ops, SparseCore 0:
  22.8 66.2 all-gather.5
  90.8 62.8 all-gather.3
  359.5 99.1 all-gather.7
where the time goes:
time: 484 us; the launch traced here: 477 us
  waiting for transfers between devices  315 us (65%)
  matrix products  86.7 us (18%)
  other arithmetic  41.4 us (9%)
  between operations  15.7 us (3%)
  starting transfers between devices  14.7 us (3%)
    ppermute x3, waiting for transfers between devices, passed_along(): return lax.ppermute(block, axis, route)  132 us
    ppermute x4, waiting for transfers between devices, passed_along_2(): lax.ppermute(x, axis, [(i, (i + by) % devices) for i in range(devices)])  74.8 us
    all_gather x1, waiting for transfers between devices, local(): lax.all_gather(local_forward(initial_state), 'cores', axis=1, tiled=True)  60.5 us
    all_gather x1, waiting for transfers between devices, local(): lax.all_gather(local_forward(heat_source), 'cores', axis=1, tiled=True)  48.2 us
    mul x3, other arithmetic, local(): current = forcing * factor  35.8 us
    dot_general x2, matrix products, local_forward(): return jnp.einsum('cz,ayz->ayc', basis_z, values, precision=HIGHEST)  21.4 us
    dot_general x8, matrix products, local(): jnp.einsum('ka,abc->kbc', edge_rows, current, precision=HIGHEST)  20.6 us
    dot_general x2, matrix products, local(): jnp.einsum('by,ayc->abc', mode_block, piece_part, precision=HIGHEST)  18.3 us
  transfers between devices with their start and end apart: 10, of which 7 were waited for; matrix products, arithmetic and copies ran while one was open for 10% of the time, Pallas kernels for 0%

commit v1 on v0

--- a/solution.py
+++ b/solution.py
@@ -4,6 +4,11 @@
 from jax.sharding import PartitionSpec as P
 
 HIGHEST = lax.Precision.HIGHEST
+
+
+def gather_over(x, name, along):
+    repeated = jnp.stack([x] * lax.axis_size(name))
+    return jnp.concatenate(lax.all_to_all(repeated, name, 0, 0), axis=along)
 
 
 def passed_along(block, axis, distance):
@@ -51,7 +56,7 @@
         return jnp.einsum("cz,ayz->ayc", basis_z, values, precision=HIGHEST)
 
     pieces = (
-        lax.all_gather(local_forward(initial_state), "cores", axis=1, tiled=True),
+        gather_over(local_forward(initial_state), "cores", 1),
         lax.all_gather(local_forward(heat_source), "cores", axis=1, tiled=True),
     )
     start_modes, source_modes = tuple(

time: 484 us -> 473 us (0.977)
  waiting for transfers between devices: 315 us -> 293 us
  local copies, waits for them, and re-layouts: 3.34 us -> 9.94 us
  starting transfers between devices: 14.7 us -> 20.6 us
  matrix products: 86.7 us -> 81.5 us
    all_to_all x0 -> x1, waiting for transfers between devices: none -> 87.1 us  [gather_over(): return jnp.concatenate(lax.all_to_all(repeated, name, 0, 0), axis=along)]
    all_gather x1 -> x0, waiting for transfers between devices: 60.5 us -> none  [local(): lax.all_gather(local_forward(initial_state), 'cores', axis=1, tiled=True)]
    all_gather x1, waiting for transfers between devices: 48.2 us -> 0.01 us  [local(): lax.all_gather(local_forward(heat_source), 'cores', axis=1, tiled=True)]
    all_to_all x0 -> x1, starting transfers between devices: none -> 5.99 us  [gather_over(): return jnp.concatenate(lax.all_to_all(repeated, name, 0, 0), axis=along)]
    reshape x0 -> x1, local copies, waits for them, and re-layouts: none -> 5.04 us  [gather_over(): return jnp.concatenate(lax.all_to_all(repeated, name, 0, 0), axis=along)]
  transfers between devices with their start and end apart: 10 -> 10, of which waited for: 7 -> 6; matrix products, arithmetic and copies ran while one was open for 10% -> 10% of each run, Pallas kernels for 0% -> 0%
where the time goes in v1:
time: 473 us; the launch traced here: 466 us
  waiting for transfers between devices  293 us (62%)
  matrix products  81.5 us (17%)
  other arithmetic  44.7 us (9%)
  starting transfers between devices  20.6 us (4%)
  between operations  16 us (3%)
  local copies, waits for them, and re-layouts  9.94 us (2%)
    ppermute x3, waiting for transfers between devices, passed_along(): return lax.ppermute(block, axis, route)  131 us
    all_to_all x1, waiting for transfers between devices, gather_over(): return jnp.concatenate(lax.all_to_all(repeated, name, 0, 0), axis=along)  87.1 us
    ppermute x4, waiting for transfers between devices, passed_along_2(): lax.ppermute(x, axis, [(i, (i + by) % devices) for i in range(devices)])  74.8 us
    mul x3, other arithmetic, local(): current = forcing * factor  36.3 us
    dot_general x8, matrix products, local(): jnp.einsum('ka,abc->kbc', edge_rows, current, precision=HIGHEST)  20.6 us
    dot_general x2, matrix products, local_forward(): return jnp.einsum('cz,ayz->ayc', basis_z, values, precision=HIGHEST)  19.2 us
    dot_general x2, matrix products, local(): jnp.einsum('by,ayc->abc', mode_block, piece_part, precision=HIGHEST)  17 us
  transfers between devices with their start and end apart: 10, of which 6 were waited for; matrix products, arithmetic and copies ran while one was open for 10% of the time, Pallas kernels for 0%

profile of v1, /device:TPU:3, one launch (start us, length us, event | category | flops | bytes accessed | tf_op | source)
XLA Modules:
  0.0 465.8 jit_solution(14394723024580338765)
XLA Ops:
  7.2 0.0 copy-start
  7.2 0.0 all-gather.3.cloned.1.call-start
  7.3 1.5 copy-done
  8.8 3.1 fusion.57
  11.9 11.0 %fusion.55 = f32[32,32,512]{2,1,0:T(8,128)} fusion(f32[32,32,512]{2,0,1:T(8,128)S(1)} %fusion.57, f32[512]{0:T(512)S(1)} %get-tuple-element.57, f32[512]{0:T(512)S(1)} %get-tuple-element.58, f32[512]{0:T(512)S(1)} %fusion.184), kind=kOutput, calls=%fused_computation.134 | convolution fusion | flops 3222011904 | bytes 4200448 | tf_op jit(solution)/shard_map/cz,ayz->ayc/dot_general | solution.py:56
  22.9 0.0 copy-start.12
  22.9 0.0 all-gather.3.cloned.1.call-update
  22.9 1.6 copy-done.12
  24.5 3.1 fusion.61
  27.6 8.2 %fusion.81 = f32[1,32,32,512]{3,2,1,0:T(8,128)S(1)} fusion(f32[32,32,512]{2,0,1:T(8,128)S(1)} %fusion.61, f32[512]{0:T(512)S(1)} %get-tuple-element.57, f32[512]{0:T(512)S(1)} %get-tuple-element.58, f32[512]{0:T(512)S(1)} %fusion.184), kind=kOutput, calls=%fused_computation.161 | convolution fusion | flops 3222011904 | bytes 4200448 | tf_op jit(solution)/shard_map/cz,ayz->ayc/dot_general | solution.py:56
  35.8 2.7 pad_maximum_fusion
  38.5 6.0 %all-to-all-start = ((f32[2,32,32,512]{3,2,1,0:T(8,128)}), f32[2,32,32,512]{3,2,1,0:T(8,128)}, u32[]{:S(2)}, u32[]{:S(2)}) async-start(f32[2,32,32,512]{3,2,1,0:T(8,128)} %pad_maximum_fusion), calls=%async_computation | async-start | bytes 8388608 | tf_op jit(solution)/shard_map/all_to_all | solution.py:11
  44.5 0.6 all-gather.5.cloned.1.call-start
  45.8 0.7 fusion.209
  46.4 0.1 cosine_multiply_fusion.5
  46.6 0.1 broadcast_add_fusion
  46.7 0.2 cosine_multiply_fusion.4
  46.9 0.1 slice_bitcast_fusion.15
  47.0 87.1 %all-to-all-done = f32[2,32,32,512]{3,2,1,0:T(8,128)} async-done(((f32[2,32,32,512]{3,2,1,0:T(8,128)}), f32[2,32,32,512]{3,2,1,0:T(8,128)}, u32[]{:S(2)}, u32[]{:S(2)}) %all-to-all-start) | async-done | bytes 4194336 | tf_op jit(solution)/shard_map/all_to_all | solution.py:11
  134.1 5.0 %copy.27 = f32[32,2,32,512]{3,2,1,0:T(8,128)} copy(f32[32,2,32,512]{3,2,0,1:T(8,128)} %bitcast.12) | data formatting | bytes 8388608 | tf_op jit(solution)/shard_map/reshape | solution.py:11
  139.2 4.3 fusion.163
  143.5 12.7 %fusion.49 = (f32[32,32,512]{2,1,0:T(8,128)}, f32[32,512,32]{1,2,0:T(8,128)}) fusion(f32[32,512,32]{1,2,0:T(8,128)S(1)} %fusion.163, f32[32,512]{1,0:T(8,128)S(1)} %get-tuple-element.16, f32[32,512]{1,0:T(8,128)S(1)} %get-tuple-element.17, f32[]{:T(128)} %bitcast.48, f32[32,512]{1,0:T(8,128)S(1)} %get-tuple-element.18, ...), kind=kOutput, calls=%fused_computation.114 | convolution fusion | flops 434110464 | bytes 11570216 | tf_op jit(solution)/shard_map/by,ayc->abc/dot_general | solution.py:64
  156.2 3.1 collective-permute-start
  159.3 45.5 %collective-permute-done = f32[32,32,512]{2,1,0:T(8,128)} collective-permute-done((f32[32,32,512]{2,1,0:T(8,128)}, f32[32,32,512]{2,1,0:T(8,128)}, u32[]{:S(2)}, u32[]{:S(2)}) %collective-permute-start) | collective-permute-done | bytes 2097184 | tf_op jit(solution)/shard_map/ppermute | solution.py:17
  204.8 11.3 %fusion.50 = f32[32,32,512]{2,1,0:T(8,128)S(1)} fusion(f32[32,32,512]{2,1,0:T(8,128)} %collective-permute-done, f32[32,512,32]{1,2,0:T(8,128)} %get-tuple-element.54, f32[32,512,32]{1,2,0:T(8,128)S(1)} %fusion.163, f32[32,512]{1,0:T(8,128)S(1)} %get-tuple-element.16, f32[32,512]{1,0:T(8,128)S(1)} %get-tuple-element.17, f32[]{:T(128)} %bitcast.48, ...), kind=kLoop, calls=%fused_computation.115 | loop fusion | flops 31981568 | bytes 9443621 | tf_op jit(solution)/shard_map/mul | solution.py:96
  216.1 3.1 collective-permute-start.1
  219.2 44.3 %collective-permute-done.1 = f32[32,32,512]{2,1,0:T(8,128)S(1)} collective-permute-done((f32[32,32,512]{2,1,0:T(8,128)S(1)}, f32[32,32,512]{2,1,0:T(8,128)S(1)}, u32[]{:S(2)}, u32[]{:S(2)}) %collective-permute-start.1) | collective-permute-done | bytes 2097184 | tf_op jit(solution)/shard_map/ppermute | solution.py:17
  263.5 0.0 copy-done.4
  263.5 10.7 %fusion.51 = f32[32,32,512]{2,1,0:T(8,128)} fusion(f32[32,32,512]{2,1,0:T(8,128)S(1)} %collective-permute-done.1, f32[32,512,32]{1,2,0:T(8,128)S(1)} %copy-done.4, f32[32,512,32]{1,2,0:T(8,128)S(1)} %fusion.163, f32[32,512]{1,0:T(8,128)S(1)} %get-tuple-element.16, f32[32,512]{1,0:T(8,128)S(1)} %get-tuple-element.17, f32[]{:T(128)} %bitcast.48, ...), kind=kLoop, calls=%fused_computation.116 | loop fusion | flops 31981568 | bytes 9443621 | tf_op jit(solution)/shard_map/mul | solution.py:96
  274.1 3.1 collective-permute-start.2
  277.9 0.8 fusion.191
  278.6 0.8 compare_bitcast_fusion.2
  279.4 41.4 %collective-permute-done.2 = f32[32,32,512]{2,1,0:T(8,128)} collective-permute-done((f32[32,32,512]{2,1,0:T(8,128)}, f32[32,32,512]{2,1,0:T(8,128)}, u32[]{:S(2)}, u32[]{:S(2)}) %collective-permute-start.2) | collective-permute-done | bytes 2097184 | tf_op jit(solution)/shard_map/ppermute | solution.py:17
  320.9 14.4 %fusion.52 = (f32[32,32,512]{2,1,0:T(8,128)S(1)}, f32[32,32,512]{2,1,0:T(8,128)}, f32[32,32,512]{2,1,0:T(8,128)}, f32[32,32,512]{2,1,0:T(8,128)}, f32[32,32,512]...) fusion(f32[32,512,32]{1,2,0:T(8,128)S(1)} %fusion.163, ...), kind=kLoop, calls=%fused_computation.117 | loop fusion | flops 31981568 | bytes 24123684 | tf_op jit(solution)/shard_map/mul | solution.py:96
  335.3 3.1 fusion.77
  338.4 9.4 %fusion.53 = f32[32,32,512]{2,1,0:T(8,128)} fusion(f32[32,32,512]{2,0,1:T(8,128)S(1)} %fusion.77, f32[512]{0:T(512)S(1)} %get-tuple-element.57, f32[512]{0:T(512)S(1)} %get-tuple-element.58, f32[512]{0:T(512)S(1)} %fusion.184), kind=kOutput, calls=%fused_computation.132 | convolution fusion | flops 3222011904 | bytes 4200448 | tf_op jit(solution)/shard_map/cz,xbc->xbz/dot_general | solution.py:132
  347.8 0.0 all-gather.5.cloned.1.call-update
  347.8 4.1 fusion.93
  352.0 2.3 fusion.99
  354.3 2.3 fusion.105
  356.6 2.3 fusion.111
  358.9 0.0 copy-start.5
  358.9 2.3 fusion.117
  361.3 2.7 fusion.123
  364.0 2.3 fusion.129
  366.3 2.3 fusion.87
  368.6 1.0 fusion.207
  369.6 0.3 copy_select_fusion.1
  369.9 3.8 collective-permute-start.3
  373.7 1.3 fusion.208
  375.0 0.2 fusion.147
  375.2 0.1 collective-permute-start.4
  375.3 0.3 copy_select_fusion
  375.6 0.6 collective-permute-start.5
  376.2 65.4 %collective-permute-done.4 = f32[8,32,512]{2,1,0:T(8,128)S(1)} collective-permute-done((f32[8,32,512]{2,1,0:T(8,128)S(1)}, f32[8,32,512]{2,1,0:T(8,128)S(1)}, u32[]{:S(2)}, u32[]{:S(2)}) %collective-permute-start.4) | collective-permute-done | bytes 524320 | tf_op jit(solution)/shard_map/ppermute | solution.py:22
  441.6 0.0 collective-permute-done.3
  441.6 0.3 fusion.144
  441.9 0.3 collective-permute-start.6
  442.2 0.0 collective-permute-done.5
  442.2 9.3 %collective-permute-done.6 = f32[8,32,512]{2,1,0:T(8,128)S(1)} collective-permute-done((f32[8,32,512]{2,1,0:T(8,128)S(1)}, f32[8,32,512]{2,1,0:T(8,128)S(1)}, u32[]{:S(2)}, u32[]{:S(2)}) %collective-permute-start.6) | collective-permute-done | bytes 524320 | tf_op jit(solution)/shard_map/ppermute | solution.py:22
  451.5 0.2 fusion.140
  451.7 0.0 copy-start.1
  451.7 1.1 maximum_bitcast_fusion
  452.8 6.0 %convolution_bitcast_fusion = f32[1,32,32,512]{3,2,1,0:T(8,128)} fusion(f32[32,64,512]{2,1,0:T(8,128)} %all-gather.5.cloned.1.call-done, f32[64,64]{1,0:T(8,128)S(1)} %cosine_multiply_fusion.4, s32[]{:T(128)S(6)} %select_n.140), kind=kOutput, calls=%fused_computation.162 | convolution fusion | flops 402653184 | bytes 6307844 | tf_op jit(solution)/shard_map/by,xbz->xyz/dot_general | solution.py:133
  (39 shorter events, 0.1 us)
Async XLA Ops:
  7.2 1.6 copy-start
  7.2 132.0 %all-gather.3.cloned.1.call-start = ((), (), s32[]{:S(2)}) async-start(), calls=%async_computation.1 | async-start | bytes 6291456 | tf_op jit(solution)/shard_map/all_gather | solution.py:60
  22.9 1.6 copy-start.12
  38.5 7.3 %copy-start.14 = (f32[8]{0:T(128)S(1)}, f32[8]{0:T(128)}, u32[]{:S(2)}) copy-start(f32[8]{0:T(128)} %param.13) | copy-start | bytes 100
  38.5 8.1 %copy-start.16 = (f32[32]{0:T(128)S(1)}, f32[32]{0:T(128)}, u32[]{:S(2)}) copy-start(f32[32]{0:T(128)} %param.17) | copy-start | bytes 388
  38.5 8.1 %copy-start.17 = (f32[32]{0:T(128)S(1)}, f32[32]{0:T(128)}, u32[]{:S(2)}) copy-start(f32[32]{0:T(128)} %param.16) | copy-start | bytes 388
  38.5 8.4 %copy-start.13 = (f32[1,2,8,32,512]{4,3,2,1,0:T(8,128)S(1)}, f32[1,2,8,32,512]{4,3,2,1,0:T(8,128)}, u32[]{:S(2)}) copy-start(f32[1,2,8,32,512]{4,3,2,1,0:T(8,128)} %param.19) | copy-start | bytes 3145732
  38.5 95.6 %all-to-all-start = ((f32[2,32,32,512]{3,2,1,0:T(8,128)}), f32[2,32,32,512]{3,2,1,0:T(8,128)}, u32[]{:S(2)}, u32[]{:S(2)}) async-start(f32[2,32,32,512]{3,2,1,0:T(8,128)} %pad_maximum_fusion), calls=%async_computation | async-start | bytes 8388608 | tf_op jit(solution)/shard_map/all_to_all | solution.py:11
  44.5 408.3 %all-gather.5.cloned.1.call-start = ((), (), s32[]{:S(2)}) async-start(), calls=%async_computation.2 | async-start | bytes 6291456 | tf_op jit(solution)/shard_map/all_gather | solution.py:136
  139.2 4.3 copy-start.15
  139.2 4.3 copy-start.11
  156.2 48.6 %collective-permute-start = (f32[32,32,512]{2,1,0:T(8,128)}, f32[32,32,512]{2,1,0:T(8,128)}, u32[]{:S(2)}, u32[]{:S(2)}) collective-permute-start(f32[32,32,512]{2,1,0:T(8,128)} %get-tuple-element.53), channel_id=1, source_target_pairs={{0,2},{2,4},{4,6},{1,3},{3,5},{5,7},{8,10},{10,12},{12,14},{9,11},... | collective-permute-start | bytes 6291464 | tf_op jit(solution)/shard_map/ppermute | solution.py:17
  204.8 58.7 %copy-start.4 = (f32[32,512,32]{1,2,0:T(8,128)S(1)}, f32[32,512,32]{1,2,0:T(8,128)}, u32[]{:S(2)}) copy-start(f32[32,512,32]{1,2,0:T(8,128)} %get-tuple-element.54) | copy-start | bytes 6291460
  216.1 47.4 %collective-permute-start.1 = (f32[32,32,512]{2,1,0:T(8,128)S(1)}, f32[32,32,512]{2,1,0:T(8,128)S(1)}, u32[]{:S(2)}, u32[]{:S(2)}) collective-permute-start(f32[32,32,512]{2,1,0:T(8,128)S(1)} %fusion.50), channel_id=1, source_target_pairs={{0,2},{2,4},{4,6},{1,3},{3,5},{5,7},{8,10},{10,12},{12,14},{9,11},... | collective-permute-start | bytes 6291464 | tf_op jit(solution)/shard_map/ppermute | solution.py:17
  274.1 46.8 %collective-permute-start.2 = (f32[32,32,512]{2,1,0:T(8,128)}, f32[32,32,512]{2,1,0:T(8,128)}, u32[]{:S(2)}, u32[]{:S(2)}) collective-permute-start(f32[32,32,512]{2,1,0:T(8,128)} %fusion.51), channel_id=1, source_target_pairs={{0,2},{2,4},{4,6},{1,3},{3,5},{5,7},{8,10},{10,12},{12,14},{9,11},... | collective-permute-start | bytes 6291464 | tf_op jit(solution)/shard_map/ppermute | solution.py:17
  335.3 3.1 copy-start.2
  347.8 4.2 copy-start.10
  347.8 6.5 %copy-start.9 = (f32[32,32,512]{2,1,0:T(8,128)S(1)}, f32[32,32,512]{2,1,0:T(8,128)}, u32[]{:S(2)}) copy-start(f32[32,32,512]{2,1,0:T(8,128)} %get-tuple-element.7) | copy-start | bytes 6291460
  352.0 4.6 copy-start.8
  354.3 4.6 copy-start.7
  356.6 4.6 copy-start.6
  358.9 5.0 %copy-start.5 = (f32[32,32,512]{2,1,0:T(8,128)S(1)}, f32[32,32,512]{2,1,0:T(8,128)}, u32[]{:S(2)}) copy-start(f32[32,32,512]{2,1,0:T(8,128)} %get-tuple-element.3) | copy-start | bytes 6291460
  361.3 5.0 %copy-start.3 = (f32[32,32,512]{2,1,0:T(8,128)S(1)}, f32[32,32,512]{2,1,0:T(8,128)}, u32[]{:S(2)}) copy-start(f32[32,32,512]{2,1,0:T(8,128)} %copy-done.2) | copy-start | bytes 6291460
  369.9 71.7 %collective-permute-start.3 = (f32[8,2,32,512]{3,2,0,1:T(8,128)S(1)}, f32[8,2,32,512]{3,2,0,1:T(8,128)S(1)}, u32[]{:S(2)}, u32[]{:S(2)}) collective-permute-start(f32[8,2,32,512]{3,2,0,1:T(8,128)S(1)} %copy_select_fusion.1), channel_id=1, source_target_pairs={{0,8},{8,16},{16,24},{24,32},{32,40},{40,48},{48,56},{56,64},{64,7... | collective-permute-start | bytes 3145736 | tf_op jit(solution)/shard_map/ppermute | solution.py:22
  375.2 66.4 %collective-permute-start.4 = (f32[8,32,512]{2,1,0:T(8,128)S(1)}, f32[8,32,512]{2,1,0:T(8,128)S(1)}, u32[]{:S(2)}, u32[]{:S(2)}) collective-permute-start(f32[8,32,512]{2,1,0:T(8,128)S(1)} %fusion.147), channel_id=1, source_target_pairs={{0,8},{8,16},{16,24},{24,32},{32,40},{40,48},{48,56},{56,64},{64,7... | collective-permute-start | bytes 1572872 | tf_op jit(solution)/shard_map/ppermute | solution.py:22
  375.6 66.6 %collective-permute-start.5 = (f32[8,2,32,512]{3,2,0,1:T(8,128)S(1)}, f32[8,2,32,512]{3,2,0,1:T(8,128)S(1)}, u32[]{:S(2)}, u32[]{:S(2)}) collective-permute-start(f32[8,2,32,512]{3,2,0,1:T(8,128)S(1)} %copy_select_fusion), channel_id=1, source_target_pairs={{0,248},{8,0},{16,8},{24,16},{32,24},{40,32},{48,40},{56,48},{64,5... | collective-permute-start | bytes 3145736 | tf_op jit(solution)/shard_map/ppermute | solution.py:22
  441.9 9.6 %collective-permute-start.6 = (f32[8,32,512]{2,1,0:T(8,128)S(1)}, f32[8,32,512]{2,1,0:T(8,128)S(1)}, u32[]{:S(2)}, u32[]{:S(2)}) collective-permute-start(f32[8,32,512]{2,1,0:T(8,128)S(1)} %get-tuple-element.44), channel_id=1, source_target_pairs={{0,248},{8,0},{16,8},{24,16},{32,24},{40,32},{48,40},{56,48},{64,5... | collective-permute-start | bytes 1572872 | tf_op jit(solution)/shard_map/ppermute | solution.py:22
  451.7 7.1 %copy-start.1 = (f32[32,32,512]{2,1,0:T(8,128)S(1)}, f32[32,32,512]{2,1,0:T(8,128)}, u32[]{:S(2)}) copy-start(f32[32,32,512]{2,1,0:T(8,128)} %param.12) | copy-start | bytes 6291460
Sparse Core Ops, SparseCore 0:
  23.0 106.2 all-gather.2
  347.9 99.5 all-gather.4
